TPU v7x, 32 devices: a whole 2x2x4 slice. The times are simulated.
32 devices in a mesh: section: 4 (over z), dp: 8 (over y, x, core).
Axes of the slice: x: 2, y: 2, z: 4, core: 2. Of those that a mesh axis runs over, the one named last changes fastest.
Arguments:
- acts: bfloat16 [4, 4, 8, 12, 16, 512], P('section', None, 'dp'), may hold values from -6 to 6
- out_grad: bfloat16 [4, 8, 12, 16, 512], P(None, 'dp'), may hold values from -6 to 6
- depth_kernel: bfloat16 [4, 3, 3, 512], P('section'), may hold values from -2 to 2
- point_weight: bfloat16 [4, 512, 512], P('section'), may hold values from -0.25 to 0.25
- bn_gain: float32 [4, 512], P('section'), may hold values from 0.15 to 0.45
Outputs:
- act_grad: bfloat16 [4, 4, 8, 12, 16, 512], P('section', None, 'dp')
- point_grad: float32 [4, 512, 512], P('section')
- kernel_grad: float32 [4, 3, 3, 512], P('section')
- gain_grad: float32 [4, 512], P('section')
- bias_grad: float32 [4, 512], P('section')
All inputs are finite; a program needn't handle non-finite values.
Results may differ from a plain program's by a relative error of at most 0.025.
Values may be sent and summed in bfloat16 or wider, within the bound.
No kernel may reach another device: no remote copies, remote signals or barrier semaphores. Data moves between devices by JAX's collectives and lax.ppermute only.
A program may use at most 64 MiB of HBM per device.

v0:
```python
import jax
import jax.numpy as jnp
from jax import lax
from jax.sharding import PartitionSpec as P

epsilon = 1e-05


def shifted(x, axis, by):
    length = lax.axis_size(axis)
    pairs = [(i, i + by) for i in range(length) if 0 <= i + by < length]
    return lax.ppermute(x, axis, pairs)


def depthwise(active, kernel):
    padded = jnp.pad(active, ((0, 0), (1, 1), (1, 1), (0, 0)))
    height, width = (active.shape[1], active.shape[2])
    summed = jnp.zeros(active.shape, jnp.float32)
    for row_off in range(3):
        for col_off in range(3):
            summed = (
                summed
                + kernel[row_off, col_off]
                * padded[:, row_off : row_off + height, col_off : col_off + width]
            )
    return summed


def depthwise_back(grad, kernel):
    padded = jnp.pad(grad, ((0, 0), (1, 1), (1, 1), (0, 0)))
    height, width = (grad.shape[1], grad.shape[2])
    summed = jnp.zeros(grad.shape, jnp.float32)
    for row_off in range(3):
        for col_off in range(3):
            summed = (
                summed
                + kernel[row_off, col_off]
                * padded[:, 2 - row_off : 2 - row_off + height, 2 - col_off : 2 - col_off + width]
            )
    return summed


def kernel_terms(active, grad):
    padded = jnp.pad(active, ((0, 0), (1, 1), (1, 1), (0, 0)))
    height, width = (active.shape[1], active.shape[2])
    table = []
    for row_off in range(3):
        line = []
        for col_off in range(3):
            line.append(
                jnp.sum(
                    padded[:, row_off : row_off + height, col_off : col_off + width] * grad,
                    axis=(0, 1, 2),
                )
            )
        table.append(jnp.stack(line))
    return jnp.stack(table)


def pick(array, slot):
    return lax.dynamic_index_in_dim(array, slot, 0, keepdims=False)


def body(acts, out_grad, depth_kernel, point_weight, bn_gain):
    sections = lax.axis_size("section")
    replicas = lax.axis_size("dp")
    my_section = lax.axis_index("section")
    micros, images, height, width, channels = acts.shape[1:]
    rows = images * height * width
    count = images * replicas * height * width
    shape = (images, height, width, channels)
    inputs = acts[0]
    kernel = depth_kernel[0].astype(jnp.float32)
    weight = point_weight[0]
    gain = bn_gain[0]
    active = jnp.maximum(inputs.astype(jnp.float32), 0.0)
    depth_out = depthwise(active.reshape(micros * images, height, width, channels), kernel).astype(
        jnp.bfloat16
    )
    depth_flat = depth_out.reshape(micros * rows, channels)
    pre_norm = jnp.dot(depth_flat, weight, preferred_element_type=jnp.float32).reshape(
        micros, rows, channels
    )
    center_sum, square_sum = lax.psum(
        (jnp.sum(pre_norm, axis=1), jnp.sum(pre_norm * pre_norm, axis=1)), "dp"
    )
    center_all = center_sum / count
    inv_all = lax.rsqrt(square_sum / count - center_all * center_all + epsilon)
    normed_all = (pre_norm - center_all[:, None, :]) * inv_all[:, None, :]
    pre_bank = jnp.zeros((micros, rows, channels), jnp.bfloat16)
    depth_bank = jnp.zeros((micros,) + shape, jnp.float32)

    def step(turn, carry):
        incoming, grads_out, gain_acc, bias_acc, point_acc, kernel_acc, pre_store, depth_store = (
            carry
        )
        micro = turn - (sections - 1 - my_section)
        valid = jnp.logical_and(micro >= 0, micro < micros)
        slot = jnp.clip(micro, 0, micros - 1)
        flag = valid.astype(jnp.float32)
        upstream = jnp.where(my_section == sections - 1, pick(out_grad, slot), incoming)
        upstream = upstream.astype(jnp.float32).reshape(rows, channels)
        normed = pick(normed_all, slot)
        inv_std = pick(inv_all, slot)
        sum_grad, sum_cross = lax.psum(
            (jnp.sum(upstream, axis=0), jnp.sum(upstream * normed, axis=0)), "dp"
        )
        pre_grad = (
            gain * inv_std * (upstream - sum_grad / count - normed * sum_cross / count)
        ).astype(jnp.bfloat16)
        depth_grad = lax.dot_general(
            pre_grad, weight, (((1,), (1,)), ((), ())), preferred_element_type=jnp.float32
        ).reshape(shape)
        input_slot = pick(inputs, slot)
        back = depthwise_back(depth_grad, kernel)
        input_grad = (upstream.reshape(shape) + jnp.where(input_slot > 0, back, 0.0)).astype(
            jnp.bfloat16
        )
        gain_acc = gain_acc + flag * sum_cross
        bias_acc = bias_acc + flag * sum_grad
        kept_pre = jnp.where(valid, pre_grad, pick(pre_store, slot))
        pre_store = lax.dynamic_update_index_in_dim(pre_store, kept_pre, slot, 0)
        kept_depth = jnp.where(valid, depth_grad, pick(depth_store, slot))
        depth_store = lax.dynamic_update_index_in_dim(depth_store, kept_depth, slot, 0)
        kept_grad = jnp.where(valid, input_grad, pick(grads_out, slot))
        grads_out = lax.dynamic_update_index_in_dim(grads_out, kept_grad, slot, 0)
        incoming = shifted(input_grad, "section", -1)
        return (
            incoming,
            grads_out,
            gain_acc,
            bias_acc,
            point_acc,
            kernel_acc,
            pre_store,
            depth_store,
        )

    start = (
        jnp.zeros(shape, jnp.bfloat16),
        jnp.zeros((micros,) + shape, jnp.bfloat16),
        jnp.zeros((channels,), jnp.float32),
        jnp.zeros((channels,), jnp.float32),
        jnp.zeros((channels, channels), jnp.float32),
        jnp.zeros((3, 3, channels), jnp.float32),
        pre_bank,
        depth_bank,
    )
    final = lax.fori_loop(0, sections + micros - 1, step, start)
    grads_out, gain_acc, bias_acc, point_acc, kernel_acc, pre_store, depth_store = final[1:]
    point_acc = lax.dot_general(
        depth_flat,
        pre_store.reshape(micros * rows, channels),
        (((0,), (0,)), ((), ())),
        preferred_element_type=jnp.float32,
    )
    kernel_acc = kernel_terms(
        active.reshape(micros * images, height, width, channels),
        depth_store.reshape(micros * images, height, width, channels),
    )
    point_sum, kernel_sum = (
        lax.psum(point_acc.astype(jnp.bfloat16), "dp").astype(jnp.float32),
        lax.psum(kernel_acc.astype(jnp.bfloat16), "dp").astype(jnp.float32),
    )
    return (grads_out[None], point_sum[None], kernel_sum[None], gain_acc[None], bias_acc[None])


def solution(mesh):
    return jax.shard_map(
        body,
        mesh=mesh,
        in_specs=(
            P("section", None, "dp", None, None, None),
            P(None, "dp", None, None, None),
            P("section", None, None, None),
            P("section", None, None),
            P("section", None),
        ),
        out_specs=(
            P("section", None, "dp", None, None, None),
            P("section", None, None),
            P("section", None, None, None),
            P("section", None),
            P("section", None),
        ),
        check_vma=False,
    )
```

profile of v0, /device:TPU:0, one launch (start us, length us, event | category | flops | bytes accessed | tf_op | source)
XLA Modules:
  0.0 283.1 jit_solution(14415372862434217522)
XLA Ops:
  8.0 1.3 maximum_bitcast_fusion
  9.3 2.2 add_convert_fusion
  11.6 1.7 fusion.40
  13.3 25.5 %all-reduce.3 = (f32[4,512]{1,0:T(4,128)S(1)}, f32[4,512]{1,0:T(4,128)S(1)}) all-reduce(f32[4,512]{1,0:T(4,128)S(1)} %get-tuple-element.436, f32[4,512]{1,0:T(4,128)S(1)} %get-tuple-element.435), channel_id=1, replica_groups=mesh['section'=4,'dp'=8] {'dp'}, use_global_device_ids=true, to_apply=%region_3.4 | all-reduce | flops 4096 | bytes 32768 | tf_op jit(solution)/shard_map/psum | solution.py:84
  38.9 1.7 subtract_multiply_fusion
  42.5 1.3 broadcast.164
  43.9 174.0 %while.26 = (s32[]{:T(128)}, bf16[1,12,16,512]{3,2,1,0:T(8,128)(2,1)S(1)}, bf16[4,1,12,16,512]{4,3,2,1,0:T(8,128)(2,1)}, f32[512]{0:T(512)S(1)}, f32[512]{0:T(51...) while((s32[]{:T(128)}, ...), condition=%wide.region_9.10_spmd.clone, body=%wide.region_4.9_spmd.clone.sunk | while | flops 105189384 | bytes 8489298 | solution.py:149
  46.0 11.8 %all-reduce.5 = (f32[512]{0:T(512)S(1)}, f32[512]{0:T(512)S(1)}) all-reduce(f32[512]{0:T(512)S(1)} %get-tuple-element.621, f32[512]{0:T(512)S(1)} %get-tuple-element.622), channel_id=1, replica_groups=mesh['section'=4,'dp'=8] {'dp'}, use_global_device_ids=true, to_apply=%region_8.8 | all-reduce | flops 1024 | bytes 8192 | tf_op jit(solution)/shard_map/while/body/eval_jaxpr/psum | solution.py:105
  58.2 2.0 bitcast_dynamic-update-slice_fusion.2
  60.2 1.3 collective-permute-start
  61.5 1.7 constant_dynamic-update-slice_fusion.2
  63.2 1.8 select_dynamic-update-slice_fusion.2
  65.0 3.7 %collective-permute-done = bf16[1,12,16,512]{3,2,1,0:T(8,128)(2,1)S(1)} collective-permute-done((bf16[1,12,16,512]{3,2,1,0:T(8,128)(2,1)S(1)}, bf16[1,12,16,512]{3,2,1,0:T(8,128)(2,1)S(1)}, u32[]{:S(2)}, u32[]{:S(2)}) %collective-permute-start) | collective-permute-done | bytes 196640 | tf_op jit(solution)/shard_map/while/body/eval_jaxpr/ppermute | solution.py:12
  70.8 11.8 %all-reduce.5 = (f32[512]{0:T(512)S(1)}, f32[512]{0:T(512)S(1)}) all-reduce(f32[512]{0:T(512)S(1)} %get-tuple-element.621, f32[512]{0:T(512)S(1)} %get-tuple-element.622), channel_id=1, replica_groups=mesh['section'=4,'dp'=8] {'dp'}, use_global_device_ids=true, to_apply=%region_8.8 | all-reduce | flops 1024 | bytes 8192 | tf_op jit(solution)/shard_map/while/body/eval_jaxpr/psum | solution.py:105
  83.0 2.0 bitcast_dynamic-update-slice_fusion.2
  86.3 1.7 constant_dynamic-update-slice_fusion.2
  88.0 1.8 select_dynamic-update-slice_fusion.2
  89.8 3.7 %collective-permute-done = bf16[1,12,16,512]{3,2,1,0:T(8,128)(2,1)S(1)} collective-permute-done((bf16[1,12,16,512]{3,2,1,0:T(8,128)(2,1)S(1)}, bf16[1,12,16,512]{3,2,1,0:T(8,128)(2,1)S(1)}, u32[]{:S(2)}, u32[]{:S(2)}) %collective-permute-start) | collective-permute-done | bytes 196640 | tf_op jit(solution)/shard_map/while/body/eval_jaxpr/ppermute | solution.py:12
  95.7 11.8 %all-reduce.5 = (f32[512]{0:T(512)S(1)}, f32[512]{0:T(512)S(1)}) all-reduce(f32[512]{0:T(512)S(1)} %get-tuple-element.621, f32[512]{0:T(512)S(1)} %get-tuple-element.622), channel_id=1, replica_groups=mesh['section'=4,'dp'=8] {'dp'}, use_global_device_ids=true, to_apply=%region_8.8 | all-reduce | flops 1024 | bytes 8192 | tf_op jit(solution)/shard_map/while/body/eval_jaxpr/psum | solution.py:105
  107.9 2.0 bitcast_dynamic-update-slice_fusion.2
  111.2 1.7 constant_dynamic-update-slice_fusion.2
  112.9 1.8 select_dynamic-update-slice_fusion.2
  114.7 3.7 %collective-permute-done = bf16[1,12,16,512]{3,2,1,0:T(8,128)(2,1)S(1)} collective-permute-done((bf16[1,12,16,512]{3,2,1,0:T(8,128)(2,1)S(1)}, bf16[1,12,16,512]{3,2,1,0:T(8,128)(2,1)S(1)}, u32[]{:S(2)}, u32[]{:S(2)}) %collective-permute-start) | collective-permute-done | bytes 196640 | tf_op jit(solution)/shard_map/while/body/eval_jaxpr/ppermute | solution.py:12
  120.5 11.8 %all-reduce.5 = (f32[512]{0:T(512)S(1)}, f32[512]{0:T(512)S(1)}) all-reduce(f32[512]{0:T(512)S(1)} %get-tuple-element.621, f32[512]{0:T(512)S(1)} %get-tuple-element.622), channel_id=1, replica_groups=mesh['section'=4,'dp'=8] {'dp'}, use_global_device_ids=true, to_apply=%region_8.8 | all-reduce | flops 1024 | bytes 8192 | tf_op jit(solution)/shard_map/while/body/eval_jaxpr/psum | solution.py:105
  132.7 2.0 bitcast_dynamic-update-slice_fusion.2
  136.0 1.7 constant_dynamic-update-slice_fusion.2
  137.7 1.8 select_dynamic-update-slice_fusion.2
  139.5 3.7 %collective-permute-done = bf16[1,12,16,512]{3,2,1,0:T(8,128)(2,1)S(1)} collective-permute-done((bf16[1,12,16,512]{3,2,1,0:T(8,128)(2,1)S(1)}, bf16[1,12,16,512]{3,2,1,0:T(8,128)(2,1)S(1)}, u32[]{:S(2)}, u32[]{:S(2)}) %collective-permute-start) | collective-permute-done | bytes 196640 | tf_op jit(solution)/shard_map/while/body/eval_jaxpr/ppermute | solution.py:12
  145.4 11.8 %all-reduce.5 = (f32[512]{0:T(512)S(1)}, f32[512]{0:T(512)S(1)}) all-reduce(f32[512]{0:T(512)S(1)} %get-tuple-element.621, f32[512]{0:T(512)S(1)} %get-tuple-element.622), channel_id=1, replica_groups=mesh['section'=4,'dp'=8] {'dp'}, use_global_device_ids=true, to_apply=%region_8.8 | all-reduce | flops 1024 | bytes 8192 | tf_op jit(solution)/shard_map/while/body/eval_jaxpr/psum | solution.py:105
  157.6 2.0 bitcast_dynamic-update-slice_fusion.2
  160.9 1.7 constant_dynamic-update-slice_fusion.2
  162.6 1.8 select_dynamic-update-slice_fusion.2
  164.4 3.7 %collective-permute-done = bf16[1,12,16,512]{3,2,1,0:T(8,128)(2,1)S(1)} collective-permute-done((bf16[1,12,16,512]{3,2,1,0:T(8,128)(2,1)S(1)}, bf16[1,12,16,512]{3,2,1,0:T(8,128)(2,1)S(1)}, u32[]{:S(2)}, u32[]{:S(2)}) %collective-permute-start) | collective-permute-done | bytes 196640 | tf_op jit(solution)/shard_map/while/body/eval_jaxpr/ppermute | solution.py:12
  170.2 11.8 %all-reduce.5 = (f32[512]{0:T(512)S(1)}, f32[512]{0:T(512)S(1)}) all-reduce(f32[512]{0:T(512)S(1)} %get-tuple-element.621, f32[512]{0:T(512)S(1)} %get-tuple-element.622), channel_id=1, replica_groups=mesh['section'=4,'dp'=8] {'dp'}, use_global_device_ids=true, to_apply=%region_8.8 | all-reduce | flops 1024 | bytes 8192 | tf_op jit(solution)/shard_map/while/body/eval_jaxpr/psum | solution.py:105
  182.4 2.0 bitcast_dynamic-update-slice_fusion.2
  185.7 1.7 constant_dynamic-update-slice_fusion.2
  187.4 1.8 select_dynamic-update-slice_fusion.2
  189.2 3.7 %collective-permute-done = bf16[1,12,16,512]{3,2,1,0:T(8,128)(2,1)S(1)} collective-permute-done((bf16[1,12,16,512]{3,2,1,0:T(8,128)(2,1)S(1)}, bf16[1,12,16,512]{3,2,1,0:T(8,128)(2,1)S(1)}, u32[]{:S(2)}, u32[]{:S(2)}) %collective-permute-start) | collective-permute-done | bytes 196640 | tf_op jit(solution)/shard_map/while/body/eval_jaxpr/ppermute | solution.py:12
  195.1 11.8 %all-reduce.5 = (f32[512]{0:T(512)S(1)}, f32[512]{0:T(512)S(1)}) all-reduce(f32[512]{0:T(512)S(1)} %get-tuple-element.621, f32[512]{0:T(512)S(1)} %get-tuple-element.622), channel_id=1, replica_groups=mesh['section'=4,'dp'=8] {'dp'}, use_global_device_ids=true, to_apply=%region_8.8 | all-reduce | flops 1024 | bytes 8192 | tf_op jit(solution)/shard_map/while/body/eval_jaxpr/psum | solution.py:105
  207.3 2.0 bitcast_dynamic-update-slice_fusion.2
  210.6 1.7 constant_dynamic-update-slice_fusion.2
  212.3 1.8 select_dynamic-update-slice_fusion.2
  214.1 3.7 %collective-permute-done = bf16[1,12,16,512]{3,2,1,0:T(8,128)(2,1)S(1)} collective-permute-done((bf16[1,12,16,512]{3,2,1,0:T(8,128)(2,1)S(1)}, bf16[1,12,16,512]{3,2,1,0:T(8,128)(2,1)S(1)}, u32[]{:S(2)}, u32[]{:S(2)}) %collective-permute-start) | collective-permute-done | bytes 196640 | tf_op jit(solution)/shard_map/while/body/eval_jaxpr/ppermute | solution.py:12
  217.8 2.9 %fusion.37 = bf16[1,512,512]{2,1,0:T(8,128)(2,1)} fusion(bf16[768,512]{1,0:T(8,128)(2,1)} %bitcast.175, bf16[768,512]{1,0:T(8,128)(2,1)} %bitcast.173), kind=kOutput, calls=%fused_computation.83 | convolution fusion | flops 402915328 | bytes 2097152 | tf_op jit(solution)/shard_map/dot_general | solution.py:151
  220.8 6.4 %fusion.28 = (bf16[512]{0:T(512)(128)(2,1)S(1)}, bf16[512]{0:T(512)(128)(2,1)S(1)}, bf16[512]{0:T(512)(128)(2,1)S(1)}, bf16[512]{0:T(512)(128)(2,1)S(1)}, bf16[5...) fusion(f32[4,1,12,16,512]{4,3,2,1,0:T(8,128)S(1)} %copy-done, ...), kind=kLoop, calls=%fused_computation.69 | loop fusion | flops 7859712 | bytes 3941376 | tf_op jit(solution)/shard_map/reduce_sum | solution.py:51
  227.4 22.5 %psum.59 = bf16[1,3,3,512]{3,0,2,1:T(2,128)(2,1)S(1)} all-reduce(bf16[1,3,3,512]{3,0,2,1:T(2,128)(2,1)S(1)} %broadcast_in_dim.73), channel_id=1, replica_groups=mesh['section'=4,'dp'=8] {'dp'}, use_global_device_ids=true, to_apply=%region_20.21 | all-reduce | flops 4608 | bytes 18432 | tf_op jit(solution)/shard_map/psum | solution.py:163
  250.6 23.5 %all-reduce.8.cloned.1.call-done = bf16[1,512,512]{2,1,0:T(8,128)(2,1)} async-done(((bf16[1,512,512]{2,1,0:T(8,128)(2,1)}), bf16[1,512,512]{2,1,0:T(8,128)(2,1)}) %all-reduce.8.cloned.1.call-update) | async-done | bytes 524304 | tf_op jit(solution)/shard_map/psum | solution.py:162
  274.1 2.1 broadcast_in_dim.72
  (109 shorter events, 28.6 us)
Async XLA Ops:
  7.2 266.9 %all-reduce.8.cloned.1.call-start = ((), (), s32[]{:S(2)}) async-start(), calls=%async_computation | async-start | bytes 1048576 | tf_op jit(solution)/shard_map/psum | solution.py:162
  9.3 4.0 %copy-start.1 = (f32[4,12,16,512]{3,2,1,0:T(8,128)}, f32[4,12,16,512]{3,2,1,0:T(8,128)S(1)}, u32[]{:S(2)}) copy-start(f32[4,12,16,512]{3,2,1,0:T(8,128)S(1)} %maximum_bitcast_fusion) | copy-start | bytes 4718596
  9.3 2.2 copy-start.2
  11.6 1.8 copy-start.4
  40.6 3.3 %copy-start.6 = (f32[1,512]{1,0:T(1,128)S(1)}, f32[1,512]{1,0:T(1,128)}, u32[]{:S(2)}) copy-start(f32[1,512]{1,0:T(1,128)} %param.11) | copy-start | bytes 6148
  60.2 8.6 %collective-permute-start = (bf16[1,12,16,512]{3,2,1,0:T(8,128)(2,1)S(1)}, bf16[1,12,16,512]{3,2,1,0:T(8,128)(2,1)S(1)}, u32[]{:S(2)}, u32[]{:S(2)}) collective-permute-start(bf16[1,12,16,512]{3,2,1,0:T(8,128)(2,1)S(1)} %get-tuple-element.631), channel_id=1, source_target_pairs={{8,0},{16,8},{24,16},{9,1},{17,9},{25,17},{10,2},{18,10},{26,18},{... | collective-permute-start | bytes 589832 | tf_op jit(solution)/shard_map/while/body/eval_jaxpr/ppermute | solution.py:12
  85.0 8.6 %collective-permute-start = (bf16[1,12,16,512]{3,2,1,0:T(8,128)(2,1)S(1)}, bf16[1,12,16,512]{3,2,1,0:T(8,128)(2,1)S(1)}, u32[]{:S(2)}, u32[]{:S(2)}) collective-permute-start(bf16[1,12,16,512]{3,2,1,0:T(8,128)(2,1)S(1)} %get-tuple-element.631), channel_id=1, source_target_pairs={{8,0},{16,8},{24,16},{9,1},{17,9},{25,17},{10,2},{18,10},{26,18},{... | collective-permute-start | bytes 589832 | tf_op jit(solution)/shard_map/while/body/eval_jaxpr/ppermute | solution.py:12
  109.9 8.6 %collective-permute-start = (bf16[1,12,16,512]{3,2,1,0:T(8,128)(2,1)S(1)}, bf16[1,12,16,512]{3,2,1,0:T(8,128)(2,1)S(1)}, u32[]{:S(2)}, u32[]{:S(2)}) collective-permute-start(bf16[1,12,16,512]{3,2,1,0:T(8,128)(2,1)S(1)} %get-tuple-element.631), channel_id=1, source_target_pairs={{8,0},{16,8},{24,16},{9,1},{17,9},{25,17},{10,2},{18,10},{26,18},{... | collective-permute-start | bytes 589832 | tf_op jit(solution)/shard_map/while/body/eval_jaxpr/ppermute | solution.py:12
  134.7 8.6 %collective-permute-start = (bf16[1,12,16,512]{3,2,1,0:T(8,128)(2,1)S(1)}, bf16[1,12,16,512]{3,2,1,0:T(8,128)(2,1)S(1)}, u32[]{:S(2)}, u32[]{:S(2)}) collective-permute-start(bf16[1,12,16,512]{3,2,1,0:T(8,128)(2,1)S(1)} %get-tuple-element.631), channel_id=1, source_target_pairs={{8,0},{16,8},{24,16},{9,1},{17,9},{25,17},{10,2},{18,10},{26,18},{... | collective-permute-start | bytes 589832 | tf_op jit(solution)/shard_map/while/body/eval_jaxpr/ppermute | solution.py:12
  159.6 8.6 %collective-permute-start = (bf16[1,12,16,512]{3,2,1,0:T(8,128)(2,1)S(1)}, bf16[1,12,16,512]{3,2,1,0:T(8,128)(2,1)S(1)}, u32[]{:S(2)}, u32[]{:S(2)}) collective-permute-start(bf16[1,12,16,512]{3,2,1,0:T(8,128)(2,1)S(1)} %get-tuple-element.631), channel_id=1, source_target_pairs={{8,0},{16,8},{24,16},{9,1},{17,9},{25,17},{10,2},{18,10},{26,18},{... | collective-permute-start | bytes 589832 | tf_op jit(solution)/shard_map/while/body/eval_jaxpr/ppermute | solution.py:12
  184.4 8.6 %collective-permute-start = (bf16[1,12,16,512]{3,2,1,0:T(8,128)(2,1)S(1)}, bf16[1,12,16,512]{3,2,1,0:T(8,128)(2,1)S(1)}, u32[]{:S(2)}, u32[]{:S(2)}) collective-permute-start(bf16[1,12,16,512]{3,2,1,0:T(8,128)(2,1)S(1)} %get-tuple-element.631), channel_id=1, source_target_pairs={{8,0},{16,8},{24,16},{9,1},{17,9},{25,17},{10,2},{18,10},{26,18},{... | collective-permute-start | bytes 589832 | tf_op jit(solution)/shard_map/while/body/eval_jaxpr/ppermute | solution.py:12
  209.3 8.6 %collective-permute-start = (bf16[1,12,16,512]{3,2,1,0:T(8,128)(2,1)S(1)}, bf16[1,12,16,512]{3,2,1,0:T(8,128)(2,1)S(1)}, u32[]{:S(2)}, u32[]{:S(2)}) collective-permute-start(bf16[1,12,16,512]{3,2,1,0:T(8,128)(2,1)S(1)} %get-tuple-element.631), channel_id=1, source_target_pairs={{8,0},{16,8},{24,16},{9,1},{17,9},{25,17},{10,2},{18,10},{26,18},{... | collective-permute-start | bytes 589832 | tf_op jit(solution)/shard_map/while/body/eval_jaxpr/ppermute | solution.py:12
  217.8 9.4 %copy-start.5 = (f32[512]{0:T(512)}, f32[512]{0:T(512)S(1)}, u32[]{:S(2)}) copy-start(f32[512]{0:T(512)S(1)} %get-tuple-element.371) | copy-start | bytes 6148
  217.8 9.4 %copy-start.7 = (f32[512]{0:T(512)}, f32[512]{0:T(512)S(1)}, u32[]{:S(2)}) copy-start(f32[512]{0:T(512)S(1)} %get-tuple-element.372) | copy-start | bytes 6148
  217.8 3.0 %copy-start = (f32[4,1,12,16,512]{4,3,2,1,0:T(8,128)S(1)}, f32[4,1,12,16,512]{4,3,2,1,0:T(8,128)}, u32[]{:S(2)}) copy-start(f32[4,1,12,16,512]{4,3,2,1,0:T(8,128)} %get-tuple-element.370) | copy-start | bytes 4718596
  217.8 3.0 %copy-start.3 = (bf16[4,1,12,16,512]{4,3,2,1,0:T(8,128)(2,1)S(1)}, bf16[4,1,12,16,512]{4,3,2,1,0:T(8,128)(2,1)}, u32[]{:S(2)}) copy-start(bf16[4,1,12,16,512]{4,3,2,1,0:T(8,128)(2,1)} %get-tuple-element.695) | copy-start | bytes 2359300
Sparse Core Ops, SparseCore 0:
  220.9 53.1 all-reduce.7
where the time goes:
time: 285 us; the launch traced here: 283 us
  blocking collectives  131 us (46%)
  other arithmetic  61.9 us (22%)
  waiting for transfers between devices  49.7 us (17%)
  between operations  14.3 us (5%)
  local copies, waits for them, and re-layouts  10.3 us (4%)
  starting transfers between devices  9 us (3%)
  matrix products  6.9 us (2%)
    psum x7, blocking collectives, step(): lax.psum((jnp.sum(upstream, axis=0), jnp.sum(upstream * normed, axis=0)),...  82.6 us
    ppermute x7, waiting for transfers between devices, shifted(): return lax.ppermute(x, axis, pairs)  26.1 us
    psum x1, blocking collectives, body(): lax.psum((jnp.sum(pre_norm, axis=1), jnp.sum(pre_norm * pre_norm, axis=1)...  25.5 us
    psum x1, waiting for transfers between devices, body(): lax.psum(point_acc.astype(jnp.bfloat16), 'dp').astype(jnp.float32)  23.5 us
    psum x1, blocking collectives, body(): lax.psum(kernel_acc.astype(jnp.bfloat16), 'dp').astype(jnp.float32)  22.5 us
    dynamic_update_slice x7, other arithmetic, step(): grads_out = lax.dynamic_update_index_in_dim(grads_out, kept_grad, slot, 0)  13.9 us
    dynamic_update_slice x7, other arithmetic, step(): lax.dynamic_update_index_in_dim(depth_store, kept_depth, slot, 0)  12.6 us
    dynamic_update_slice x7, other arithmetic, step(): pre_store = lax.dynamic_update_index_in_dim(pre_store, kept_pre, slot, 0)  12.1 us
  transfers between devices with their start and end apart: 8, of which 8 were waited for; matrix products, arithmetic and copies ran while one was open for 11% of the time, Pallas kernels for 0%

commit v1 on v0

--- a/solution.py
+++ b/solution.py
@@ -2,6 +2,7 @@
 import jax.numpy as jnp
 from jax import lax
 from jax.sharding import PartitionSpec as P
+from jax.lax import all_gather
 
 epsilon = 1e-05
 
@@ -160,7 +161,7 @@
     )
     point_sum, kernel_sum = (
         lax.psum(point_acc.astype(jnp.bfloat16), "dp").astype(jnp.float32),
-        lax.psum(kernel_acc.astype(jnp.bfloat16), "dp").astype(jnp.float32),
+        jnp.sum(all_gather(kernel_acc.astype(jnp.bfloat16), "dp"), 0).astype(jnp.float32),
     )
     return (grads_out[None], point_sum[None], kernel_sum[None], gain_acc[None], bias_acc[None])
 

time: 285 us -> 285 us (level)
  blocking collectives: 131 us -> 116 us
  waiting for transfers between devices: 49.7 us -> 64 us
    psum x1 -> x0, blocking collectives: 22.5 us -> none  [body(): lax.psum(kernel_acc.astype(jnp.bfloat16), 'dp').astype(jnp.float32)]
    psum x1, waiting for transfers between devices: 23.5 us -> 37.9 us  [body(): lax.psum(point_acc.astype(jnp.bfloat16), 'dp').astype(jnp.float32)]
    all_gather x0 -> x1, blocking collectives: none -> 8.27 us  [body(): all_gather(kernel_acc.astype(jnp.bfloat16), 'dp')]
where the time goes in v1:
time: 285 us; the launch traced here: 283 us
  blocking collectives  116 us (41%)
  waiting for transfers between devices  64 us (22%)
  other arithmetic  61.4 us (22%)
  between operations  14.3 us (5%)
  local copies, waits for them, and re-layouts  10.9 us (4%)
  starting transfers between devices  9 us (3%)
  matrix products  6.9 us (2%)
    psum x7, blocking collectives, step(): lax.psum((jnp.sum(upstream, axis=0), jnp.sum(upstream * normed, axis=0)),...  82.6 us
    psum x1, waiting for transfers between devices, body(): lax.psum(point_acc.astype(jnp.bfloat16), 'dp').astype(jnp.float32)  37.9 us
    ppermute x7, waiting for transfers between devices, shifted(): return lax.ppermute(x, axis, pairs)  26.1 us
    psum x1, blocking collectives, body(): lax.psum((jnp.sum(pre_norm, axis=1), jnp.sum(pre_norm * pre_norm, axis=1)...  25.5 us
    dynamic_update_slice x7, other arithmetic, step(): grads_out = lax.dynamic_update_index_in_dim(grads_out, kept_grad, slot, 0)  13.9 us
    dynamic_update_slice x7, other arithmetic, step(): lax.dynamic_update_index_in_dim(depth_store, kept_depth, slot, 0)  12.6 us
    dynamic_update_slice x7, other arithmetic, step(): pre_store = lax.dynamic_update_index_in_dim(pre_store, kept_pre, slot, 0)  12.1 us
    ppermute x7, starting transfers between devices, shifted(): return lax.ppermute(x, axis, pairs)  8.96 us
  transfers between devices with their start and end apart: 8, of which 8 were waited for; matrix products, arithmetic and copies ran while one was open for 11% of the time, Pallas kernels for 0%

profile of v1, /device:TPU:0, one launch (start us, length us, event | category | flops | bytes accessed | tf_op | source)
XLA Modules:
  0.0 283.2 jit_solution(156822704427930493)
XLA Ops:
  8.0 1.3 maximum_bitcast_fusion
  9.3 2.2 add_convert_fusion
  11.6 1.7 fusion.40
  13.3 25.5 %all-reduce.3 = (f32[4,512]{1,0:T(4,128)S(1)}, f32[4,512]{1,0:T(4,128)S(1)}) all-reduce(f32[4,512]{1,0:T(4,128)S(1)} %get-tuple-element.436, f32[4,512]{1,0:T(4,128)S(1)} %get-tuple-element.435), channel_id=1, replica_groups=mesh['section'=4,'dp'=8] {'dp'}, use_global_device_ids=true, to_apply=%region_3.4 | all-reduce | flops 4096 | bytes 32768 | tf_op jit(solution)/shard_map/psum | solution.py:85
  38.9 1.7 subtract_multiply_fusion
  42.5 1.3 broadcast.164
  43.9 174.0 %while.26 = (s32[]{:T(128)}, bf16[1,12,16,512]{3,2,1,0:T(8,128)(2,1)S(1)}, bf16[4,1,12,16,512]{4,3,2,1,0:T(8,128)(2,1)}, f32[512]{0:T(512)S(1)}, f32[512]{0:T(51...) while((s32[]{:T(128)}, ...), condition=%wide.region_9.10_spmd.clone, body=%wide.region_4.9_spmd.clone.sunk | while | flops 105189384 | bytes 8489298 | solution.py:150
  46.0 11.8 %all-reduce.5 = (f32[512]{0:T(512)S(1)}, f32[512]{0:T(512)S(1)}) all-reduce(f32[512]{0:T(512)S(1)} %get-tuple-element.621, f32[512]{0:T(512)S(1)} %get-tuple-element.622), channel_id=1, replica_groups=mesh['section'=4,'dp'=8] {'dp'}, use_global_device_ids=true, to_apply=%region_8.8 | all-reduce | flops 1024 | bytes 8192 | tf_op jit(solution)/shard_map/while/body/eval_jaxpr/psum | solution.py:106
  58.2 2.0 bitcast_dynamic-update-slice_fusion.2
  60.2 1.3 collective-permute-start
  61.5 1.7 constant_dynamic-update-slice_fusion.2
  63.2 1.8 select_dynamic-update-slice_fusion.2
  65.0 3.7 %collective-permute-done = bf16[1,12,16,512]{3,2,1,0:T(8,128)(2,1)S(1)} collective-permute-done((bf16[1,12,16,512]{3,2,1,0:T(8,128)(2,1)S(1)}, bf16[1,12,16,512]{3,2,1,0:T(8,128)(2,1)S(1)}, u32[]{:S(2)}, u32[]{:S(2)}) %collective-permute-start) | collective-permute-done | bytes 196640 | tf_op jit(solution)/shard_map/while/body/eval_jaxpr/ppermute | solution.py:13
  70.8 11.8 %all-reduce.5 = (f32[512]{0:T(512)S(1)}, f32[512]{0:T(512)S(1)}) all-reduce(f32[512]{0:T(512)S(1)} %get-tuple-element.621, f32[512]{0:T(512)S(1)} %get-tuple-element.622), channel_id=1, replica_groups=mesh['section'=4,'dp'=8] {'dp'}, use_global_device_ids=true, to_apply=%region_8.8 | all-reduce | flops 1024 | bytes 8192 | tf_op jit(solution)/shard_map/while/body/eval_jaxpr/psum | solution.py:106
  83.0 2.0 bitcast_dynamic-update-slice_fusion.2
  86.3 1.7 constant_dynamic-update-slice_fusion.2
  88.0 1.8 select_dynamic-update-slice_fusion.2
  89.8 3.7 %collective-permute-done = bf16[1,12,16,512]{3,2,1,0:T(8,128)(2,1)S(1)} collective-permute-done((bf16[1,12,16,512]{3,2,1,0:T(8,128)(2,1)S(1)}, bf16[1,12,16,512]{3,2,1,0:T(8,128)(2,1)S(1)}, u32[]{:S(2)}, u32[]{:S(2)}) %collective-permute-start) | collective-permute-done | bytes 196640 | tf_op jit(solution)/shard_map/while/body/eval_jaxpr/ppermute | solution.py:13
  95.7 11.8 %all-reduce.5 = (f32[512]{0:T(512)S(1)}, f32[512]{0:T(512)S(1)}) all-reduce(f32[512]{0:T(512)S(1)} %get-tuple-element.621, f32[512]{0:T(512)S(1)} %get-tuple-element.622), channel_id=1, replica_groups=mesh['section'=4,'dp'=8] {'dp'}, use_global_device_ids=true, to_apply=%region_8.8 | all-reduce | flops 1024 | bytes 8192 | tf_op jit(solution)/shard_map/while/body/eval_jaxpr/psum | solution.py:106
  107.9 2.0 bitcast_dynamic-update-slice_fusion.2
  111.2 1.7 constant_dynamic-update-slice_fusion.2
  112.9 1.8 select_dynamic-update-slice_fusion.2
  114.7 3.7 %collective-permute-done = bf16[1,12,16,512]{3,2,1,0:T(8,128)(2,1)S(1)} collective-permute-done((bf16[1,12,16,512]{3,2,1,0:T(8,128)(2,1)S(1)}, bf16[1,12,16,512]{3,2,1,0:T(8,128)(2,1)S(1)}, u32[]{:S(2)}, u32[]{:S(2)}) %collective-permute-start) | collective-permute-done | bytes 196640 | tf_op jit(solution)/shard_map/while/body/eval_jaxpr/ppermute | solution.py:13
  120.5 11.8 %all-reduce.5 = (f32[512]{0:T(512)S(1)}, f32[512]{0:T(512)S(1)}) all-reduce(f32[512]{0:T(512)S(1)} %get-tuple-element.621, f32[512]{0:T(512)S(1)} %get-tuple-element.622), channel_id=1, replica_groups=mesh['section'=4,'dp'=8] {'dp'}, use_global_device_ids=true, to_apply=%region_8.8 | all-reduce | flops 1024 | bytes 8192 | tf_op jit(solution)/shard_map/while/body/eval_jaxpr/psum | solution.py:106
  132.7 2.0 bitcast_dynamic-update-slice_fusion.2
  136.0 1.7 constant_dynamic-update-slice_fusion.2
  137.7 1.8 select_dynamic-update-slice_fusion.2
  139.5 3.7 %collective-permute-done = bf16[1,12,16,512]{3,2,1,0:T(8,128)(2,1)S(1)} collective-permute-done((bf16[1,12,16,512]{3,2,1,0:T(8,128)(2,1)S(1)}, bf16[1,12,16,512]{3,2,1,0:T(8,128)(2,1)S(1)}, u32[]{:S(2)}, u32[]{:S(2)}) %collective-permute-start) | collective-permute-done | bytes 196640 | tf_op jit(solution)/shard_map/while/body/eval_jaxpr/ppermute | solution.py:13
  145.4 11.8 %all-reduce.5 = (f32[512]{0:T(512)S(1)}, f32[512]{0:T(512)S(1)}) all-reduce(f32[512]{0:T(512)S(1)} %get-tuple-element.621, f32[512]{0:T(512)S(1)} %get-tuple-element.622), channel_id=1, replica_groups=mesh['section'=4,'dp'=8] {'dp'}, use_global_device_ids=true, to_apply=%region_8.8 | all-reduce | flops 1024 | bytes 8192 | tf_op jit(solution)/shard_map/while/body/eval_jaxpr/psum | solution.py:106
  157.6 2.0 bitcast_dynamic-update-slice_fusion.2
  160.9 1.7 constant_dynamic-update-slice_fusion.2
  162.6 1.8 select_dynamic-update-slice_fusion.2
  164.4 3.7 %collective-permute-done = bf16[1,12,16,512]{3,2,1,0:T(8,128)(2,1)S(1)} collective-permute-done((bf16[1,12,16,512]{3,2,1,0:T(8,128)(2,1)S(1)}, bf16[1,12,16,512]{3,2,1,0:T(8,128)(2,1)S(1)}, u32[]{:S(2)}, u32[]{:S(2)}) %collective-permute-start) | collective-permute-done | bytes 196640 | tf_op jit(solution)/shard_map/while/body/eval_jaxpr/ppermute | solution.py:13
  170.2 11.8 %all-reduce.5 = (f32[512]{0:T(512)S(1)}, f32[512]{0:T(512)S(1)}) all-reduce(f32[512]{0:T(512)S(1)} %get-tuple-element.621, f32[512]{0:T(512)S(1)} %get-tuple-element.622), channel_id=1, replica_groups=mesh['section'=4,'dp'=8] {'dp'}, use_global_device_ids=true, to_apply=%region_8.8 | all-reduce | flops 1024 | bytes 8192 | tf_op jit(solution)/shard_map/while/body/eval_jaxpr/psum | solution.py:106
  182.4 2.0 bitcast_dynamic-update-slice_fusion.2
  185.7 1.7 constant_dynamic-update-slice_fusion.2
  187.4 1.8 select_dynamic-update-slice_fusion.2
  189.2 3.7 %collective-permute-done = bf16[1,12,16,512]{3,2,1,0:T(8,128)(2,1)S(1)} collective-permute-done((bf16[1,12,16,512]{3,2,1,0:T(8,128)(2,1)S(1)}, bf16[1,12,16,512]{3,2,1,0:T(8,128)(2,1)S(1)}, u32[]{:S(2)}, u32[]{:S(2)}) %collective-permute-start) | collective-permute-done | bytes 196640 | tf_op jit(solution)/shard_map/while/body/eval_jaxpr/ppermute | solution.py:13
  195.1 11.8 %all-reduce.5 = (f32[512]{0:T(512)S(1)}, f32[512]{0:T(512)S(1)}) all-reduce(f32[512]{0:T(512)S(1)} %get-tuple-element.621, f32[512]{0:T(512)S(1)} %get-tuple-element.622), channel_id=1, replica_groups=mesh['section'=4,'dp'=8] {'dp'}, use_global_device_ids=true, to_apply=%region_8.8 | all-reduce | flops 1024 | bytes 8192 | tf_op jit(solution)/shard_map/while/body/eval_jaxpr/psum | solution.py:106
  207.3 2.0 bitcast_dynamic-update-slice_fusion.2
  210.6 1.7 constant_dynamic-update-slice_fusion.2
  212.3 1.8 select_dynamic-update-slice_fusion.2
  214.1 3.7 %collective-permute-done = bf16[1,12,16,512]{3,2,1,0:T(8,128)(2,1)S(1)} collective-permute-done((bf16[1,12,16,512]{3,2,1,0:T(8,128)(2,1)S(1)}, bf16[1,12,16,512]{3,2,1,0:T(8,128)(2,1)S(1)}, u32[]{:S(2)}, u32[]{:S(2)}) %collective-permute-start) | collective-permute-done | bytes 196640 | tf_op jit(solution)/shard_map/while/body/eval_jaxpr/ppermute | solution.py:13
  217.8 2.9 %fusion.37 = bf16[1,512,512]{2,1,0:T(8,128)(2,1)} fusion(bf16[768,512]{1,0:T(8,128)(2,1)} %bitcast.175, bf16[768,512]{1,0:T(8,128)(2,1)} %bitcast.173), kind=kOutput, calls=%fused_computation.83 | convolution fusion | flops 402915328 | bytes 2097152 | tf_op jit(solution)/shard_map/dot_general | solution.py:152
  220.8 6.4 %fusion.28 = (bf16[512]{0:T(512)(128)(2,1)S(1)}, bf16[512]{0:T(512)(128)(2,1)S(1)}, bf16[512]{0:T(512)(128)(2,1)S(1)}, bf16[512]{0:T(512)(128)(2,1)S(1)}, bf16[5...) fusion(f32[4,1,12,16,512]{4,3,2,1,0:T(8,128)S(1)} %copy-done, ...), kind=kLoop, calls=%fused_computation.69 | loop fusion | flops 7859712 | bytes 3941376 | tf_op jit(solution)/shard_map/reduce_sum | solution.py:52
  227.4 8.3 %all_gather.4 = bf16[8,3,3,512]{3,2,1,0:T(4,128)(2,1)S(1)} all-gather(bf16[1,3,3,512]{3,2,1,0:T(4,128)(2,1)S(1)} %pad_maximum_fusion), channel_id=1, replica_groups=mesh['section'=4,'dp'=8] {'dp'}, dimensions={0}, use_global_device_ids=true | all-gather | bytes 82944 | tf_op jit(solution)/shard_map/all_gather | solution.py:164
  236.3 37.9 %all-reduce.8.cloned.1.call-done = bf16[1,512,512]{2,1,0:T(8,128)(2,1)} async-done(((bf16[1,512,512]{2,1,0:T(8,128)(2,1)}), bf16[1,512,512]{2,1,0:T(8,128)(2,1)}) %all-reduce.8.cloned.1.call-update) | async-done | bytes 524304 | tf_op jit(solution)/shard_map/psum | solution.py:163
  274.2 2.1 broadcast_in_dim.67
  (109 shorter events, 28.6 us)
Async XLA Ops:
  7.2 267.0 %all-reduce.8.cloned.1.call-start = ((), (), s32[]{:S(2)}) async-start(), calls=%async_computation | async-start | bytes 1048576 | tf_op jit(solution)/shard_map/psum | solution.py:163
  9.3 4.0 %copy-start.1 = (f32[4,12,16,512]{3,2,1,0:T(8,128)}, f32[4,12,16,512]{3,2,1,0:T(8,128)S(1)}, u32[]{:S(2)}) copy-start(f32[4,12,16,512]{3,2,1,0:T(8,128)S(1)} %maximum_bitcast_fusion) | copy-start | bytes 4718596
  9.3 2.2 copy-start.2
  11.6 1.8 copy-start.4
  40.6 3.3 %copy-start.6 = (f32[1,512]{1,0:T(1,128)S(1)}, f32[1,512]{1,0:T(1,128)}, u32[]{:S(2)}) copy-start(f32[1,512]{1,0:T(1,128)} %param.11) | copy-start | bytes 6148
  60.2 8.6 %collective-permute-start = (bf16[1,12,16,512]{3,2,1,0:T(8,128)(2,1)S(1)}, bf16[1,12,16,512]{3,2,1,0:T(8,128)(2,1)S(1)}, u32[]{:S(2)}, u32[]{:S(2)}) collective-permute-start(bf16[1,12,16,512]{3,2,1,0:T(8,128)(2,1)S(1)} %get-tuple-element.631), channel_id=1, source_target_pairs={{8,0},{16,8},{24,16},{9,1},{17,9},{25,17},{10,2},{18,10},{26,18},{... | collective-permute-start | bytes 589832 | tf_op jit(solution)/shard_map/while/body/eval_jaxpr/ppermute | solution.py:13
  85.0 8.6 %collective-permute-start = (bf16[1,12,16,512]{3,2,1,0:T(8,128)(2,1)S(1)}, bf16[1,12,16,512]{3,2,1,0:T(8,128)(2,1)S(1)}, u32[]{:S(2)}, u32[]{:S(2)}) collective-permute-start(bf16[1,12,16,512]{3,2,1,0:T(8,128)(2,1)S(1)} %get-tuple-element.631), channel_id=1, source_target_pairs={{8,0},{16,8},{24,16},{9,1},{17,9},{25,17},{10,2},{18,10},{26,18},{... | collective-permute-start | bytes 589832 | tf_op jit(solution)/shard_map/while/body/eval_jaxpr/ppermute | solution.py:13
  109.9 8.6 %collective-permute-start = (bf16[1,12,16,512]{3,2,1,0:T(8,128)(2,1)S(1)}, bf16[1,12,16,512]{3,2,1,0:T(8,128)(2,1)S(1)}, u32[]{:S(2)}, u32[]{:S(2)}) collective-permute-start(bf16[1,12,16,512]{3,2,1,0:T(8,128)(2,1)S(1)} %get-tuple-element.631), channel_id=1, source_target_pairs={{8,0},{16,8},{24,16},{9,1},{17,9},{25,17},{10,2},{18,10},{26,18},{... | collective-permute-start | bytes 589832 | tf_op jit(solution)/shard_map/while/body/eval_jaxpr/ppermute | solution.py:13
  134.7 8.6 %collective-permute-start = (bf16[1,12,16,512]{3,2,1,0:T(8,128)(2,1)S(1)}, bf16[1,12,16,512]{3,2,1,0:T(8,128)(2,1)S(1)}, u32[]{:S(2)}, u32[]{:S(2)}) collective-permute-start(bf16[1,12,16,512]{3,2,1,0:T(8,128)(2,1)S(1)} %get-tuple-element.631), channel_id=1, source_target_pairs={{8,0},{16,8},{24,16},{9,1},{17,9},{25,17},{10,2},{18,10},{26,18},{... | collective-permute-start | bytes 589832 | tf_op jit(solution)/shard_map/while/body/eval_jaxpr/ppermute | solution.py:13
  159.6 8.6 %collective-permute-start = (bf16[1,12,16,512]{3,2,1,0:T(8,128)(2,1)S(1)}, bf16[1,12,16,512]{3,2,1,0:T(8,128)(2,1)S(1)}, u32[]{:S(2)}, u32[]{:S(2)}) collective-permute-start(bf16[1,12,16,512]{3,2,1,0:T(8,128)(2,1)S(1)} %get-tuple-element.631), channel_id=1, source_target_pairs={{8,0},{16,8},{24,16},{9,1},{17,9},{25,17},{10,2},{18,10},{26,18},{... | collective-permute-start | bytes 589832 | tf_op jit(solution)/shard_map/while/body/eval_jaxpr/ppermute | solution.py:13
  184.4 8.6 %collective-permute-start = (bf16[1,12,16,512]{3,2,1,0:T(8,128)(2,1)S(1)}, bf16[1,12,16,512]{3,2,1,0:T(8,128)(2,1)S(1)}, u32[]{:S(2)}, u32[]{:S(2)}) collective-permute-start(bf16[1,12,16,512]{3,2,1,0:T(8,128)(2,1)S(1)} %get-tuple-element.631), channel_id=1, source_target_pairs={{8,0},{16,8},{24,16},{9,1},{17,9},{25,17},{10,2},{18,10},{26,18},{... | collective-permute-start | bytes 589832 | tf_op jit(solution)/shard_map/while/body/eval_jaxpr/ppermute | solution.py:13
  209.3 8.6 %collective-permute-start = (bf16[1,12,16,512]{3,2,1,0:T(8,128)(2,1)S(1)}, bf16[1,12,16,512]{3,2,1,0:T(8,128)(2,1)S(1)}, u32[]{:S(2)}, u32[]{:S(2)}) collective-permute-start(bf16[1,12,16,512]{3,2,1,0:T(8,128)(2,1)S(1)} %get-tuple-element.631), channel_id=1, source_target_pairs={{8,0},{16,8},{24,16},{9,1},{17,9},{25,17},{10,2},{18,10},{26,18},{... | collective-permute-start | bytes 589832 | tf_op jit(solution)/shard_map/while/body/eval_jaxpr/ppermute | solution.py:13
  217.8 9.4 %copy-start.5 = (f32[512]{0:T(512)}, f32[512]{0:T(512)S(1)}, u32[]{:S(2)}) copy-start(f32[512]{0:T(512)S(1)} %get-tuple-element.371) | copy-start | bytes 6148
  217.8 9.4 %copy-start.7 = (f32[512]{0:T(512)}, f32[512]{0:T(512)S(1)}, u32[]{:S(2)}) copy-start(f32[512]{0:T(512)S(1)} %get-tuple-element.372) | copy-start | bytes 6148
  217.8 3.0 %copy-start = (f32[4,1,12,16,512]{4,3,2,1,0:T(8,128)S(1)}, f32[4,1,12,16,512]{4,3,2,1,0:T(8,128)}, u32[]{:S(2)}) copy-start(f32[4,1,12,16,512]{4,3,2,1,0:T(8,128)} %get-tuple-element.370) | copy-start | bytes 4718596
  217.8 3.0 %copy-start.3 = (bf16[4,1,12,16,512]{4,3,2,1,0:T(8,128)(2,1)S(1)}, bf16[4,1,12,16,512]{4,3,2,1,0:T(8,128)(2,1)}, u32[]{:S(2)}) copy-start(bf16[4,1,12,16,512]{4,3,2,1,0:T(8,128)(2,1)} %get-tuple-element.695) | copy-start | bytes 2359300
Sparse Core Ops, SparseCore 0:
  220.9 53.2 all-reduce.7
